TPU v7x, 32 devices: a whole 2x2x4 slice. The times are simulated.
32 devices in a mesh: fsdp: 8 (over y, x, core), tp: 4 (over z).
Axes of the slice: x: 2, y: 2, z: 4, core: 2. Of those that a mesh axis runs over, the one named last changes fastest.
Arguments:
- layer_input: bfloat16 [24576, 512], P(('fsdp', 'tp')), may hold values from -6 to 6
- segment_ids: int32 [24, 1024], P('fsdp'), may hold values from 0 to 15, never falling along the last dimension, each value on 1 to 512 neighbouring positions
- valid_mask: int32 [24576], P(('fsdp', 'tp')), may hold values from 0 to 1, as said below
- teacher: bfloat16 [24576, 512], P(('fsdp', 'tp')), may hold values from -6 to 6
- cotangent: bfloat16 [24576, 512], P(('fsdp', 'tp')), may hold values from -6 to 6
- ln1_gain: bfloat16 [512], P('fsdp'), may hold values from 0.099609375 to 1.8984375
- ln1_bias: bfloat16 [512], P('fsdp'), may hold values from -1.75 to 1.75
- w_q: bfloat16 [512, 512], P('fsdp', 'tp'), may hold values from -0.25 to 0.25
- w_k: bfloat16 [512, 512], P('fsdp', 'tp'), may hold values from -0.25 to 0.25
- w_v: bfloat16 [512, 512], P('fsdp', 'tp'), may hold values from -0.25 to 0.25
- b_q: bfloat16 [8, 64], P('tp', 'fsdp'), may hold values from -3 to 3
- b_v: bfloat16 [8, 64], P('tp', 'fsdp'), may hold values from -3 to 3
- w_o: bfloat16 [512, 512], P('tp', 'fsdp'), may hold values from -1 to 1
- b_o: bfloat16 [512], P('fsdp'), may hold values from -3 to 3
- ln2_gain: bfloat16 [512], P('fsdp'), may hold values from 0.099609375 to 1.8984375
- ln2_bias: bfloat16 [512], P('fsdp'), may hold values from -1.75 to 1.75
- w_up: bfloat16 [512, 2048], P('fsdp', 'tp'), may hold values from -0.25 to 0.25
- b_up: bfloat16 [32, 64], P('tp', 'fsdp'), may hold values from -3 to 3
- w_down: bfloat16 [2048, 512], P('tp', 'fsdp'), may hold values from -0.25 to 0.25
- b_down: bfloat16 [512], P('fsdp'), may hold values from -3 to 3
Outputs:
- layer_out: bfloat16 [24576, 512], P(('fsdp', 'tp'))
- loss: float32 [], replicated
- grad_layer_input: float32 [24576, 512], P(('fsdp', 'tp'))
- grad_ln1_gain: float32 [512], P('fsdp')
- grad_ln1_bias: float32 [512], P('fsdp')
- grad_w_q: float32 [512, 512], P('fsdp', 'tp')
- grad_w_k: float32 [512, 512], P('fsdp', 'tp')
- grad_w_v: float32 [512, 512], P('fsdp', 'tp')
- grad_b_q: float32 [8, 64], P('tp', 'fsdp')
- grad_b_v: float32 [8, 64], P('tp', 'fsdp')
- grad_w_o: float32 [512, 512], P('tp', 'fsdp')
- grad_b_o: float32 [512], P('fsdp')
- grad_ln2_gain: float32 [512], P('fsdp')
- grad_ln2_bias: float32 [512], P('fsdp')
- grad_w_up: float32 [512, 2048], P('fsdp', 'tp')
- grad_b_up: float32 [32, 64], P('tp', 'fsdp')
- grad_w_down: float32 [2048, 512], P('tp', 'fsdp')
- grad_b_down: float32 [512], P('fsdp')
Inputs may be any that keep to these rules, and one draw needn't show every extreme that they name: `segment_ids`: in each sequence the ids never fall, each document holds 1 to 512 positions, and one holds exactly 512. `valid_mask`: the first token of every sequence is 1.
All inputs are finite; a program needn't handle non-finite values.
Results may differ from a plain program's by a relative error of at most 0.014.
Values may be sent and summed in bfloat16 or wider, within the bound.
No kernel may reach another device: no remote copies, remote signals or barrier semaphores. Data moves between devices by JAX's collectives and lax.ppermute only.
A program may use at most 128 MiB of HBM per device.

v0:
```python
import jax
import jax.numpy as jnp
from jax import lax
from jax.sharding import PartitionSpec as P

D = 512
HD = 64
LEN = 1024


def layer_norm(values, gains, offsets):
    center = values - jnp.mean(values, axis=-1, keepdims=True)
    spread = jnp.mean(center * center, axis=-1, keepdims=True)
    return center * lax.rsqrt(spread + 1e-05) * gains + offsets


def quick_gelu(values):
    return values * jax.nn.sigmoid(1.702 * values)


def block_scores(query_block, key_seq, segment_seq, first_row):
    block_rows = query_block.shape[0]
    query_place = first_row + jnp.arange(block_rows, dtype=jnp.int32)
    key_place = jnp.arange(key_seq.shape[0], dtype=jnp.int32)
    query_segment = lax.dynamic_slice_in_dim(segment_seq, first_row, block_rows)
    allowed = (query_segment[:, None] == segment_seq[None, :]) & (
        key_place[None, :] <= query_place[:, None]
    )
    raw_scores = jnp.einsum(
        "qhd,khd->hqk", query_block, key_seq, preferred_element_type=jnp.float32
    ) * HD ** (-0.5)
    return jnp.where(allowed[None], raw_scores, -1e30)


def forward_sequence(inputs):
    query_seq, key_seq, value_seq, segment_seq = inputs

    def forward_one_block(element):
        block_index, query_block = element
        scores = block_scores(query_block, key_seq, segment_seq, block_index * query_block.shape[0])
        row_max = jnp.max(scores, axis=-1, keepdims=True)
        exponent = jnp.exp(scores - row_max)
        row_sum = jnp.sum(exponent, axis=-1, keepdims=True)
        weights = (exponent / row_sum).astype(jnp.bfloat16)
        attended = jnp.einsum(
            "hqk,khd->qhd", weights, value_seq, preferred_element_type=jnp.float32
        )
        return (attended.astype(jnp.bfloat16), (row_max + jnp.log(row_sum))[..., 0])

    return lax.map(forward_one_block, (jnp.arange(query_seq.shape[0], dtype=jnp.int32), query_seq))


def backward_sequence(inputs):
    query_seq, key_seq, value_seq, segment_seq, total_seq, grad_out_seq = inputs
    zero_grads = jnp.zeros(key_seq.shape, jnp.float32)

    def backward_one_block(carried, element):
        grad_keys, grad_values = carried
        block_index, query_block, total_block, grad_block = element
        scores = block_scores(query_block, key_seq, segment_seq, block_index * query_block.shape[0])
        weights = jnp.exp(scores - total_block[..., None])
        grad_values = grad_values + jnp.einsum(
            "hqk,qhd->khd",
            weights.astype(jnp.bfloat16),
            grad_block,
            preferred_element_type=jnp.float32,
        )
        grad_weights = jnp.einsum(
            "qhd,khd->hqk", grad_block, value_seq, preferred_element_type=jnp.float32
        )
        grad_scores = (
            weights * (grad_weights - jnp.sum(weights * grad_weights, axis=-1, keepdims=True))
        ).astype(jnp.bfloat16)
        grad_query = jnp.einsum(
            "hqk,khd->qhd", grad_scores, key_seq, preferred_element_type=jnp.float32
        ) * HD ** (-0.5)
        grad_keys = grad_keys + jnp.einsum(
            "hqk,qhd->khd", grad_scores, query_block, preferred_element_type=jnp.float32
        ) * HD ** (-0.5)
        return ((grad_keys, grad_values), grad_query.astype(jnp.bfloat16))

    (grad_keys, grad_values), grad_queries = lax.scan(
        backward_one_block,
        (zero_grads, zero_grads),
        (jnp.arange(query_seq.shape[0], dtype=jnp.int32), query_seq, total_seq, grad_out_seq),
    )
    return (grad_queries, grad_keys.astype(jnp.bfloat16), grad_values.astype(jnp.bfloat16))


def local(
    layer_input,
    segment_ids,
    valid_mask,
    teacher,
    cotangent,
    ln1_gain,
    ln1_bias,
    w_q,
    w_k,
    w_v,
    b_q,
    b_v,
    w_o,
    b_o,
    ln2_gain,
    ln2_bias,
    w_up,
    b_up,
    w_down,
    b_down,
):
    fsdp_size = lax.axis_size("fsdp")
    tensor_size = lax.axis_size("tp")
    local_rows = layer_input.shape[0]
    (
        gain_one,
        bias_one,
        query_w,
        key_w,
        value_w,
        query_b,
        value_b,
        out_w,
        out_b,
        gain_two,
        bias_two,
        upper_w,
        upper_b,
        lower_w,
        lower_b,
    ) = (
        lax.all_gather(ln1_gain, "fsdp", axis=0, tiled=True),
        lax.all_gather(ln1_bias, "fsdp", axis=0, tiled=True),
        lax.all_gather(w_q, "fsdp", axis=0, tiled=True),
        lax.all_gather(w_k, "fsdp", axis=0, tiled=True),
        lax.all_gather(w_v, "fsdp", axis=0, tiled=True),
        lax.all_gather(b_q, "fsdp", axis=1, tiled=True),
        lax.all_gather(b_v, "fsdp", axis=1, tiled=True),
        lax.all_gather(w_o, "fsdp", axis=1, tiled=True),
        lax.all_gather(b_o, "fsdp", axis=0, tiled=True),
        lax.all_gather(ln2_gain, "fsdp", axis=0, tiled=True),
        lax.all_gather(ln2_bias, "fsdp", axis=0, tiled=True),
        lax.all_gather(w_up, "fsdp", axis=0, tiled=True),
        lax.all_gather(b_up, "fsdp", axis=1, tiled=True),
        lax.all_gather(w_down, "fsdp", axis=1, tiled=True),
        lax.all_gather(b_down, "fsdp", axis=0, tiled=True),
    )
    mask_float = valid_mask.astype(jnp.float32)
    valid_total = lax.psum(jnp.sum(mask_float), ("fsdp", "tp"))
    tokens_all = local_rows * fsdp_size * tensor_size
    input_float = layer_input.astype(jnp.float32)
    gain_first = gain_one.astype(jnp.float32)
    bias_first = bias_one.astype(jnp.float32)
    gain_second = gain_two.astype(jnp.float32)
    bias_second = bias_two.astype(jnp.float32)
    normed_one = layer_norm(input_float, gain_first, bias_first).astype(jnp.bfloat16)
    head_count = query_w.shape[1] // HD
    rows_one = lax.all_gather(normed_one, "tp", axis=0, tiled=True)
    queries = (
        jnp.dot(rows_one, query_w, preferred_element_type=jnp.float32)
        + query_b.reshape(-1).astype(jnp.float32)
    ).astype(jnp.bfloat16)
    keys_all = jnp.dot(rows_one, key_w, preferred_element_type=jnp.float32).astype(jnp.bfloat16)
    values_all = (
        jnp.dot(rows_one, value_w, preferred_element_type=jnp.float32)
        + value_b.reshape(-1).astype(jnp.float32)
    ).astype(jnp.bfloat16)
    seq_count = segment_ids.shape[0]
    block_rows = min(512, LEN)
    block_count = LEN // block_rows
    shaped_queries = queries.reshape(seq_count, block_count, block_rows, head_count, HD)
    shaped_keys = keys_all.reshape(seq_count, LEN, head_count, HD)
    shaped_values = values_all.reshape(seq_count, LEN, head_count, HD)
    attended, log_totals = lax.map(
        forward_sequence, (shaped_queries, shaped_keys, shaped_values, segment_ids)
    )
    attended = attended.reshape(-1, head_count * HD)
    attention = lax.psum_scatter(
        jnp.dot(attended, out_w, preferred_element_type=jnp.float32).astype(jnp.bfloat16),
        "tp",
        scatter_dimension=0,
        tiled=True,
    ).astype(jnp.float32)
    hidden_one = input_float + attention + out_b.astype(jnp.float32)
    normed_two = layer_norm(hidden_one, gain_second, bias_second).astype(jnp.bfloat16)
    rows_two = lax.all_gather(normed_two, "tp", axis=0, tiled=True)
    pre_act = jnp.dot(rows_two, upper_w, preferred_element_type=jnp.float32) + upper_b.reshape(
        -1
    ).astype(jnp.float32)
    activated = quick_gelu(pre_act).astype(jnp.bfloat16)
    branch = lax.psum_scatter(
        jnp.dot(activated, lower_w, preferred_element_type=jnp.float32).astype(jnp.bfloat16),
        "tp",
        scatter_dimension=0,
        tiled=True,
    ).astype(jnp.float32)
    out_full = hidden_one + branch + lower_b.astype(jnp.float32)
    difference = out_full - teacher.astype(jnp.float32)
    square_part = jnp.sum(mask_float * jnp.mean(difference * difference, axis=-1))
    grad_out = (
        cotangent.astype(jnp.float32) + tokens_all / valid_total * mask_float[:, None] * difference
    )
    grad_lower_bias = jnp.sum(grad_out, axis=0)
    grad_out_low = grad_out.astype(jnp.bfloat16)
    grad_rows = lax.all_gather(grad_out_low, "tp", axis=0, tiled=True)
    grad_hidden_units = jnp.einsum(
        "nd,fd->nf", grad_rows, lower_w, preferred_element_type=jnp.float32
    )
    grad_lower = jnp.einsum("nf,nd->fd", activated, grad_rows, preferred_element_type=jnp.float32)
    gelu_value, gelu_pull = jax.vjp(quick_gelu, pre_act)
    grad_pre = gelu_pull(grad_hidden_units)[0].astype(jnp.bfloat16)
    grad_upper = jnp.einsum("nd,nf->df", rows_two, grad_pre, preferred_element_type=jnp.float32)
    grad_upper_bias = jnp.sum(grad_pre, axis=0, dtype=jnp.float32).reshape(upper_b.shape)
    grad_normed_two = lax.psum_scatter(
        jnp.einsum("nf,df->nd", grad_pre, upper_w, preferred_element_type=jnp.float32).astype(
            jnp.bfloat16
        ),
        "tp",
        scatter_dimension=0,
        tiled=True,
    ).astype(jnp.float32)
    norm_value, second_pull = jax.vjp(layer_norm, hidden_one, gain_second, bias_second)
    grad_hidden_norm, grad_gain_second, grad_bias_second = second_pull(grad_normed_two)
    grad_hidden = grad_out + grad_hidden_norm
    grad_out_bias = jnp.sum(grad_hidden, axis=0)
    grad_attn_low = grad_hidden.astype(jnp.bfloat16)
    grad_attn_rows = lax.all_gather(grad_attn_low, "tp", axis=0, tiled=True)
    grad_out_w = jnp.einsum(
        "nc,nd->cd", attended, grad_attn_rows, preferred_element_type=jnp.float32
    )
    grad_attended = jnp.einsum(
        "nd,cd->nc", grad_attn_rows, out_w, preferred_element_type=jnp.float32
    ).astype(jnp.bfloat16)
    grad_queries, grad_keys, grad_values = lax.map(
        backward_sequence,
        (
            shaped_queries,
            shaped_keys,
            shaped_values,
            segment_ids,
            log_totals,
            grad_attended.reshape(seq_count, block_count, block_rows, head_count, HD),
        ),
    )
    flat_queries = grad_queries.reshape(-1, head_count * HD)
    flat_keys = grad_keys.reshape(-1, head_count * HD)
    flat_values = grad_values.reshape(-1, head_count * HD)
    grad_query_w = jnp.einsum(
        "nd,nc->dc", rows_one, flat_queries, preferred_element_type=jnp.float32
    )
    grad_key_w = jnp.einsum("nd,nc->dc", rows_one, flat_keys, preferred_element_type=jnp.float32)
    grad_value_w = jnp.einsum(
        "nd,nc->dc", rows_one, flat_values, preferred_element_type=jnp.float32
    )
    grad_query_b = jnp.sum(flat_queries, axis=0, dtype=jnp.float32).reshape(query_b.shape)
    grad_value_b = jnp.sum(flat_values, axis=0, dtype=jnp.float32).reshape(value_b.shape)
    stacked_grads = jnp.concatenate((flat_queries, flat_keys, flat_values), axis=1)
    stacked_weights = jnp.concatenate((query_w, key_w, value_w), axis=1)
    grad_normed_one = lax.psum_scatter(
        jnp.einsum(
            "nc,dc->nd", stacked_grads, stacked_weights, preferred_element_type=jnp.float32
        ).astype(jnp.bfloat16),
        "tp",
        scatter_dimension=0,
        tiled=True,
    ).astype(jnp.float32)
    first_value, first_pull = jax.vjp(layer_norm, input_float, gain_first, bias_first)
    grad_input_norm, grad_gain_first, grad_bias_first = first_pull(grad_normed_one)
    grad_input = grad_hidden + grad_input_norm
    summed = lax.psum(
        (
            square_part,
            grad_gain_first,
            grad_bias_first,
            grad_out_bias,
            grad_gain_second,
            grad_bias_second,
            grad_lower_bias,
        ),
        ("fsdp", "tp"),
    )
    piece_size = D // fsdp_size
    piece_start = lax.axis_index("fsdp") * piece_size

    def own_piece(vector):
        return lax.dynamic_slice_in_dim(vector, piece_start, piece_size)

    loss = 0.5 * summed[0] / valid_total
    grad_wq, grad_wk, grad_wv, grad_bq, grad_bv, grad_wo, grad_wu, grad_bu, grad_wd = (
        lax.psum_scatter(
            grad_query_w.astype(jnp.bfloat16), "fsdp", scatter_dimension=0, tiled=True
        ).astype(jnp.float32),
        lax.psum_scatter(
            grad_key_w.astype(jnp.bfloat16), "fsdp", scatter_dimension=0, tiled=True
        ).astype(jnp.float32),
        lax.psum_scatter(
            grad_value_w.astype(jnp.bfloat16), "fsdp", scatter_dimension=0, tiled=True
        ).astype(jnp.float32),
        lax.psum_scatter(
            grad_query_b.astype(jnp.bfloat16), "fsdp", scatter_dimension=1, tiled=True
        ).astype(jnp.float32),
        lax.psum_scatter(
            grad_value_b.astype(jnp.bfloat16), "fsdp", scatter_dimension=1, tiled=True
        ).astype(jnp.float32),
        lax.psum_scatter(
            grad_out_w.astype(jnp.bfloat16), "fsdp", scatter_dimension=1, tiled=True
        ).astype(jnp.float32),
        lax.psum_scatter(
            grad_upper.astype(jnp.bfloat16), "fsdp", scatter_dimension=0, tiled=True
        ).astype(jnp.float32),
        lax.psum_scatter(
            grad_upper_bias.astype(jnp.bfloat16), "fsdp", scatter_dimension=1, tiled=True
        ).astype(jnp.float32),
        lax.psum_scatter(
            grad_lower.astype(jnp.bfloat16), "fsdp", scatter_dimension=1, tiled=True
        ).astype(jnp.float32),
    )
    return (
        out_full.astype(jnp.bfloat16),
        loss,
        grad_input,
        own_piece(summed[1]),
        own_piece(summed[2]),
        grad_wq,
        grad_wk,
        grad_wv,
        grad_bq,
        grad_bv,
        grad_wo,
        own_piece(summed[3]),
        own_piece(summed[4]),
        own_piece(summed[5]),
        grad_wu,
        grad_bu,
        grad_wd,
        own_piece(summed[6]),
    )


def solution(mesh):
    placed = (
        P(("fsdp", "tp"), None),
        P("fsdp", None),
        P(("fsdp", "tp")),
        P(("fsdp", "tp"), None),
        P(("fsdp", "tp"), None),
        P("fsdp"),
        P("fsdp"),
        P("fsdp", "tp"),
        P("fsdp", "tp"),
        P("fsdp", "tp"),
        P("tp", "fsdp"),
        P("tp", "fsdp"),
        P("tp", "fsdp"),
        P("fsdp"),
        P("fsdp"),
        P("fsdp"),
        P("fsdp", "tp"),
        P("tp", "fsdp"),
        P("tp", "fsdp"),
        P("fsdp"),
    )
    return jax.shard_map(
        local,
        mesh=mesh,
        in_specs=placed,
        out_specs=(
            P(("fsdp", "tp"), None),
            P(),
            P(("fsdp", "tp"), None),
            P("fsdp"),
            P("fsdp"),
            P("fsdp", "tp"),
            P("fsdp", "tp"),
            P("fsdp", "tp"),
            P("tp", "fsdp"),
            P("tp", "fsdp"),
            P("tp", "fsdp"),
            P("fsdp"),
            P("fsdp"),
            P("fsdp"),
            P("fsdp", "tp"),
            P("tp", "fsdp"),
            P("tp", "fsdp"),
            P("fsdp"),
        ),
        check_vma=False,
    )
```

profile of v0, /device:TPU:0, one launch (start us, length us, event | category | flops | bytes accessed | tf_op | source)
XLA Modules:
  0.0 948.7 jit_solution(11095047475518688719)
XLA Ops:
  14.4 16.0 %all-reduce.11 = (bf16[512]{0:T(512)(128)(2,1)}, bf16[512]{0:T(512)(128)(2,1)}, bf16[512]{0:T(512)(128)(2,1)}, bf16[512]{0:T(512)(128)(2,1)S(1)}, bf16[512]{0:T(512)(128)(2,1)S(1)}, /*index=5*/bf16[512]{0:T(512)(128)(2,1)}) all-reduce(bf16[512]{0:T(512)(128)(2,1)S(1)} %dynamic-update-slice.5, ...), channel_id=1, replica_groups=mesh['fsdp'=8,'tp'=4] {'fsdp'}, use_global_device_ids=true, to_apply=%add.5 | all-reduce | flops 3072 | bytes 12288
  35.8 7.7 all-gather
  43.7 8.8 all-gather.1
  52.6 8.2 all_gather.60
  60.8 9.3 all_gather.62
  70.1 8.2 all_gather.63
  78.2 10.2 %all_gather.65 = bf16[128,512]{0,1:T(8,128)(2,1)} all-gather(bf16[128,64]{0,1:T(8,128)(2,1)S(1)} %copy-done.51), channel_id=1, replica_groups=mesh['fsdp'=8,'tp'=4] {'fsdp'}, dimensions={1}, use_global_device_ids=true | all-gather | bytes 147456 | tf_op jit(solution)/shard_map/all_gather | solution.py:139
  88.5 10.3 %all-gather.7.cloned.1.call-done = bf16[3072,512]{1,0:T(8,128)(2,1)} async-done(((bf16[768,512]{1,0:T(8,128)(2,1)}), bf16[3072,512]{1,0:T(8,128)(2,1)}) %all-gather.7.cloned.1.call-update) | async-done | bytes 3145744 | tf_op jit(solution)/shard_map/all_gather | solution.py:158
  98.8 3.8 fusion.49
  102.5 4.2 reshape.349
  106.8 4.7 copy.106
  113.3 3.9 reshape.351
  117.2 4.7 copy.108
  123.8 4.0 reshape.350
  127.8 3.5 copy.107
  131.4 47.3 %while.54 = (s32[]{:T(128)}, bf16[3,2,512,2,64]{2,1,0,4,3:T(2,128)(2,1)}, f32[3,2,2,512]{3,2,1,0:T(2,128)}, bf16[3,2,512,2,64]{2,4,3,1,0:T(8,128)(2,1)S(1)}, s32...) while((s32[]{:T(128)}, ...), condition=%wide.region_7.8_spmd, body=%wide.region_2.7_spmd.sunk | while | flops 282656256 | bytes 17635796 | solution.py:174
  132.2 13.3 %while.57 = (s32[]{:T(128)}, bf16[2,512,2,64]{1,3,2,0:T(8,128)(2,1)S(1)}, f32[2,2,512]{2,1,0:T(2,128)S(1)}, s32[2]{0:T(128)S(1)}, s32[1024]{0:T(1024)S(1)}, /*in...) while((s32[]{:T(128)}, ...), condition=%wide.region_6.6_spmd, body=%wide.region_3.5_spmd.sunk | while | flops 282656256 | bytes 15513803 | solution.py:50
  148.0 13.3 %while.57 = (s32[]{:T(128)}, bf16[2,512,2,64]{1,3,2,0:T(8,128)(2,1)S(1)}, f32[2,2,512]{2,1,0:T(2,128)S(1)}, s32[2]{0:T(128)S(1)}, s32[1024]{0:T(1024)S(1)}, /*in...) while((s32[]{:T(128)}, ...), condition=%wide.region_6.6_spmd, body=%wide.region_3.5_spmd.sunk | while | flops 282656256 | bytes 15513803 | solution.py:50
  163.7 13.3 %while.57 = (s32[]{:T(128)}, bf16[2,512,2,64]{1,3,2,0:T(8,128)(2,1)S(1)}, f32[2,2,512]{2,1,0:T(2,128)S(1)}, s32[2]{0:T(128)S(1)}, s32[1024]{0:T(1024)S(1)}, /*in...) while((s32[]{:T(128)}, ...), condition=%wide.region_6.6_spmd, body=%wide.region_3.5_spmd.sunk | while | flops 282656256 | bytes 15513803 | solution.py:50
  184.9 58.4 %reduce-scatter.14.cloned.1.call-done = bf16[768,512]{1,0:T(8,128)(2,1)} async-done(((bf16[3072,512]{1,0:T(8,128)(2,1)}), bf16[768,512]{1,0:T(8,128)(2,1)}) %reduce-scatter.14.cloned.1.call-update) | async-done | bytes 786448 | tf_op jit(solution)/shard_map/reduce_scatter | solution.py:178
  246.8 8.9 all_gather.71
  255.8 10.8 %all_gather.70 = bf16[512,512]{1,0:T(8,128)(2,1)} all-gather(bf16[64,512]{1,0:T(8,128)(2,1)S(1)} %copy-done.38), channel_id=1, replica_groups=mesh['fsdp'=8,'tp'=4] {'fsdp'}, dimensions={0}, use_global_device_ids=true | all-gather | bytes 589824 | tf_op jit(solution)/shard_map/all_gather | solution.py:143
  266.6 9.9 %all_gather.72 = bf16[512,512]{0,1:T(8,128)(2,1)} all-gather(bf16[512,64]{0,1:T(8,128)(2,1)S(1)} %copy-done.39), channel_id=1, replica_groups=mesh['fsdp'=8,'tp'=4] {'fsdp'}, dimensions={1}, use_global_device_ids=true | all-gather | bytes 589824 | tf_op jit(solution)/shard_map/all_gather | solution.py:145
  276.6 33.8 %all-gather.9.cloned.1.call-done = bf16[3072,512]{1,0:T(8,128)(2,1)} async-done(((bf16[768,512]{1,0:T(8,128)(2,1)}), bf16[3072,512]{1,0:T(8,128)(2,1)}) %all-gather.9.cloned.1.call-update) | async-done | bytes 3145744 | tf_op jit(solution)/shard_map/all_gather | solution.py:186
  310.4 7.4 multiply_convert_fusion.1
  319.4 3.6 convolution_convert_fusion.2
  324.3 42.1 %psum.57 = f32[]{:T(128)} all-reduce(f32[]{:T(128)} %convert_reduce_fusion.3), channel_id=1, replica_groups=mesh['fsdp'=8,'tp'=4] {'fsdp','tp'}, use_global_device_ids=true, to_apply=%region_16.17 | all-reduce | flops 1 | bytes 8 | tf_op jit(solution)/shard_map/psum | solution.py:149
  367.1 15.9 %reduce-scatter.16.cloned.1.call-done = bf16[768,512]{1,0:T(8,128)(2,1)} async-done(((bf16[3072,512]{1,0:T(8,128)(2,1)}), bf16[768,512]{1,0:T(8,128)(2,1)}) %reduce-scatter.16.cloned.1.call-update) | async-done | bytes 786448 | tf_op jit(solution)/shard_map/reduce_scatter | solution.py:191
  388.3 63.5 %all-gather.11.cloned.1.call-done = bf16[3072,512]{1,0:T(8,128)(2,1)} async-done(((bf16[768,512]{1,0:T(8,128)(2,1)}), bf16[3072,512]{1,0:T(8,128)(2,1)}) %all-gather.11.cloned.1.call-update) | async-done | bytes 3145744 | tf_op jit(solution)/shard_map/all_gather | solution.py:205
  451.8 8.7 fusion.87
  462.2 3.6 convolution_convert_fusion.1
  465.9 59.0 %reduce-scatter.18.cloned.1.call-done = bf16[768,512]{1,0:T(8,128)(2,1)} async-done(((bf16[3072,512]{1,0:T(8,128)(2,1)}), bf16[768,512]{1,0:T(8,128)(2,1)}) %reduce-scatter.18.cloned.1.call-update) | async-done | bytes 786448 | tf_op jit(solution)/shard_map/reduce_scatter | solution.py:214
  534.4 5.5 convolution_convert_fusion.6
  540.0 6.0 convolution_convert_fusion.7
  546.0 52.0 %all-gather.13.cloned.1.call-done = bf16[3072,512]{1,0:T(8,128)(2,1)} async-done(((bf16[768,512]{1,0:T(8,128)(2,1)}), bf16[3072,512]{1,0:T(8,128)(2,1)}) %all-gather.13.cloned.1.call-update) | async-done | bytes 3145744 | tf_op jit(solution)/shard_map/all_gather | solution.py:227
  598.0 3.8 convolution_convert_fusion.4
  601.8 3.4 reshape.339
  607.9 69.2 %while.56 = (s32[]{:T(128)}, bf16[3,2,512,2,64]{2,4,3,1,0:T(8,128)(2,1)}, bf16[3,1024,2,64]{1,3,2,0:T(8,128)(2,1)}, bf16[3,1024,2,64]{1,3,2,0:T(8,128)(2,1)}, bf...) while((s32[]{:T(128)}, ...), condition=%wide.region_24.25_spmd, body=%wide.region_20.24_spmd.sunk | while | flops 689438208 | bytes 45550196 | solution.py:234
  610.6 17.6 %while.58 = (s32[]{:T(128)}, f32[1024,2,64]{0,2,1:T(8,128)S(1)}, f32[1024,2,64]{0,2,1:T(8,128)}, bf16[2,512,2,64]{1,3,2,0:T(8,128)(2,1)S(1)}, bf16[2,512,2,64]{1...) while((s32[]{:T(128)}, f32[1024,2,64]{0,2,1:T(8,128)S(1)}, ...), condition=%wide.region_23.23_spmd.clone, body=%wide.region_21.22_spmd.clone.sunk | while | flops 689176064 | bytes 41330992 | solution.py:82
  633.7 17.6 %while.58 = (s32[]{:T(128)}, f32[1024,2,64]{0,2,1:T(8,128)S(1)}, f32[1024,2,64]{0,2,1:T(8,128)}, bf16[2,512,2,64]{1,3,2,0:T(8,128)(2,1)S(1)}, bf16[2,512,2,64]{1...) while((s32[]{:T(128)}, f32[1024,2,64]{0,2,1:T(8,128)S(1)}, ...), condition=%wide.region_23.23_spmd.clone, body=%wide.region_21.22_spmd.clone.sunk | while | flops 689176064 | bytes 41330992 | solution.py:82
  656.8 17.6 %while.58 = (s32[]{:T(128)}, f32[1024,2,64]{0,2,1:T(8,128)S(1)}, f32[1024,2,64]{0,2,1:T(8,128)}, bf16[2,512,2,64]{1,3,2,0:T(8,128)(2,1)S(1)}, bf16[2,512,2,64]{1...) while((s32[]{:T(128)}, f32[1024,2,64]{0,2,1:T(8,128)S(1)}, ...), condition=%wide.region_23.23_spmd.clone, body=%wide.region_21.22_spmd.clone.sunk | while | flops 689176064 | bytes 41330992 | solution.py:82
  695.6 5.1 convolution_convert_fusion
  705.8 13.7 %all-reduce.10 = (bf16[2,64]{1,0:T(2,128)(2,1)S(1)}, bf16[2,64]{1,0:T(2,128)(2,1)S(1)}, bf16[8,64]{1,0:T(8,128)(2,1)S(1)}) all-reduce(bf16[2,64]{1,0:T(2,128)(2,1)S(1)} %reduce_sum.233, bf16[2,64]{1,0:T(2,128)(2,1)S(1)} %reduce_sum.234, bf16[8,64]{1,0:T(8,128)(2,1)S(1)} %convert_element_type.247), channel_id=9, replica_groups=mesh['fsdp'=8,'tp'=4] {'fsdp'}, use_global_device_ids=true, to_apply=%region_36.37.clone | all-reduce | flops 768 | bytes 3072
  722.1 33.2 %reduce-scatter.22.cloned.1.call-done = bf16[64,128]{1,0:T(8,128)(2,1)} async-done(((bf16[512,128]{1,0:T(8,128)(2,1)}), bf16[64,128]{1,0:T(8,128)(2,1)}) %reduce-scatter.22.cloned.1.call-update) | async-done | bytes 16400 | tf_op jit(solution)/shard_map/reduce_scatter | solution.py:290
  756.6 34.9 %reduce-scatter.26.cloned.1.call-done = bf16[64,128]{1,0:T(8,128)(2,1)} async-done(((bf16[512,128]{1,0:T(8,128)(2,1)}), bf16[64,128]{1,0:T(8,128)(2,1)}) %reduce-scatter.26.cloned.1.call-update) | async-done | bytes 16400 | tf_op jit(solution)/shard_map/reduce_scatter | solution.py:296
  792.9 35.3 %reduce-scatter.24.cloned.1.call-done = bf16[64,128]{1,0:T(8,128)(2,1)} async-done(((bf16[512,128]{1,0:T(8,128)(2,1)}), bf16[64,128]{1,0:T(8,128)(2,1)}) %reduce-scatter.24.cloned.1.call-update) | async-done | bytes 16400 | tf_op jit(solution)/shard_map/reduce_scatter | solution.py:293
  829.6 61.1 %reduce-scatter.20.cloned.1.call-done = bf16[768,512]{1,0:T(8,128)(2,1)} async-done(((bf16[3072,512]{1,0:T(8,128)(2,1)}), bf16[768,512]{1,0:T(8,128)(2,1)}) %reduce-scatter.20.cloned.1.call-update) | async-done | bytes 786448 | tf_op jit(solution)/shard_map/reduce_scatter | solution.py:259
  893.4 40.6 %all-reduce.9 = (f32[]{:T(128)}, f32[512]{0:T(512)S(1)}, f32[512]{0:T(512)S(1)}, f32[512]{0:T(512)S(1)}, f32[512]{0:T(512)S(1)}, /*index=5*/f32[512]{0:T(512)S(1)}, f32[512]{0:T(512)S(1)}) all-reduce(f32[]{:T(128)} %multiply_reduce_fusion.3, f32[512]{0:T(512)S(1)} %get-tuple-element.340, ...), channel_id=1, replica_groups=mesh['fsdp'=8,'tp'=4] {'fsdp','tp'}, use_global_device_ids=true, to_apply=%region_14.15 | all-reduce | flops 3073 | bytes 24584 | tf_op jit(solution)/shard_map/psum | solution.py:270
  (450 shorter events, 192.5 us)
Async XLA Ops:
  7.2 27.3 %copy-start = (bf16[768,512]{1,0:T(8,128)(2,1)S(1)}, bf16[768,512]{1,0:T(8,128)(2,1)}, u32[]{:S(2)}) copy-start(bf16[768,512]{1,0:T(8,128)(2,1)} %param.28) | copy-start | bytes 2359300
  7.2 28.6 %copy-start.63 = (bf16[2,8]{1,0:T(2,128)(2,1)S(1)}, bf16[2,8]{1,0:T(2,128)(2,1)}, u32[]{:S(2)}) copy-start(bf16[2,8]{1,0:T(2,128)(2,1)} %param.38) | copy-start | bytes 100
  7.2 36.5 %copy-start.64 = (bf16[2,8]{1,0:T(2,128)(2,1)S(1)}, bf16[2,8]{1,0:T(2,128)(2,1)}, u32[]{:S(2)}) copy-start(bf16[2,8]{1,0:T(2,128)(2,1)} %param.39) | copy-start | bytes 100
  7.2 45.4 %copy-start.48 = (bf16[64,128]{1,0:T(8,128)(2,1)S(1)}, bf16[64,128]{1,0:T(8,128)(2,1)}, u32[]{:S(2)}) copy-start(bf16[64,128]{1,0:T(8,128)(2,1)} %param.35) | copy-start | bytes 49156
  7.2 91.5 %all-gather.7.cloned.1.call-start = ((), (), s32[]{:S(2)}) async-start(), calls=%async_computation.10 | async-start | bytes 3932160 | tf_op jit(solution)/shard_map/all_gather | solution.py:158
  30.4 30.4 %copy-start.49 = (bf16[64,128]{1,0:T(8,128)(2,1)S(1)}, bf16[64,128]{1,0:T(8,128)(2,1)}, u32[]{:S(2)}) copy-start(bf16[64,128]{1,0:T(8,128)(2,1)} %param.36) | copy-start | bytes 49156
  30.4 39.7 %copy-start.50 = (bf16[64,128]{1,0:T(8,128)(2,1)S(1)}, bf16[64,128]{1,0:T(8,128)(2,1)}, u32[]{:S(2)}) copy-start(bf16[64,128]{1,0:T(8,128)(2,1)} %param.37) | copy-start | bytes 49156
  30.4 47.8 %copy-start.51 = (bf16[128,64]{0,1:T(8,128)(2,1)S(1)}, bf16[128,64]{0,1:T(8,128)(2,1)}, u32[]{:S(2)}) copy-start(bf16[128,64]{0,1:T(8,128)(2,1)} %param.40) | copy-start | bytes 49156
  35.7 207.5 %reduce-scatter.14.cloned.1.call-start = ((), (), s32[]{:S(2)}) async-start(), calls=%async_computation.11 | async-start | bytes 3932160 | tf_op jit(solution)/shard_map/reduce_scatter | solution.py:178
  60.8 38.0 %copy-start.27 = (bf16[512,128]{1,0:T(8,128)(2,1)}, bf16[512,128]{1,0:T(8,128)(2,1)S(1)}, u32[]{:S(2)}) copy-start(bf16[512,128]{1,0:T(8,128)(2,1)S(1)} %all_gather.60) | copy-start | bytes 393220
  70.1 51.9 %copy-start.29 = (bf16[512,128]{1,0:T(8,128)(2,1)}, bf16[512,128]{1,0:T(8,128)(2,1)S(1)}, u32[]{:S(2)}) copy-start(bf16[512,128]{1,0:T(8,128)(2,1)S(1)} %all_gather.62) | copy-start | bytes 393220
  78.2 33.2 %copy-start.31 = (bf16[512,128]{1,0:T(8,128)(2,1)}, bf16[512,128]{1,0:T(8,128)(2,1)S(1)}, u32[]{:S(2)}) copy-start(bf16[512,128]{1,0:T(8,128)(2,1)S(1)} %all_gather.63) | copy-start | bytes 393220
  102.5 8.9 copy-start.3
  123.8 7.5 copy-start.7
  123.8 7.5 copy-start.8
  123.8 7.5 copy-start.37
  131.4 50.1 %copy-start.25 = (bf16[128,512]{0,1:T(8,128)(2,1)S(1)}, bf16[128,512]{0,1:T(8,128)(2,1)}, u32[]{:S(2)}) copy-start(bf16[128,512]{0,1:T(8,128)(2,1)} %all_gather.65) | copy-start | bytes 393220
  184.2 59.1 %copy-start.1 = (bf16[768,512]{1,0:T(8,128)(2,1)S(1)}, bf16[768,512]{1,0:T(8,128)(2,1)}, u32[]{:S(2)}) copy-start(bf16[768,512]{1,0:T(8,128)(2,1)} %param.28) | copy-start | bytes 2359300
  184.2 126.2 %all-gather.9.cloned.1.call-start = ((), (), s32[]{:S(2)}) async-start(), calls=%async_computation.12 | async-start | bytes 3932160 | tf_op jit(solution)/shard_map/all_gather | solution.py:186
  244.8 11.0 %copy-start.38 = (bf16[64,512]{1,0:T(8,128)(2,1)S(1)}, bf16[64,512]{1,0:T(8,128)(2,1)}, u32[]{:S(2)}) copy-start(bf16[64,512]{1,0:T(8,128)(2,1)} %param.44) | copy-start | bytes 196612
  245.3 21.3 %copy-start.39 = (bf16[512,64]{0,1:T(8,128)(2,1)S(1)}, bf16[512,64]{0,1:T(8,128)(2,1)}, u32[]{:S(2)}) copy-start(bf16[512,64]{0,1:T(8,128)(2,1)} %param.46) | copy-start | bytes 196612
  246.7 136.3 %reduce-scatter.16.cloned.1.call-start = ((), (), s32[]{:S(2)}) async-start(), calls=%async_computation.13 | async-start | bytes 3932160 | tf_op jit(solution)/shard_map/reduce_scatter | solution.py:191
  310.4 9.0 copy-start.34
  323.0 43.4 %copy-start.59 = (bf16[512]{0:T(512)(128)(2,1)S(1)}, bf16[512]{0:T(512)(128)(2,1)}, u32[]{:S(2)}) copy-start(bf16[512]{0:T(512)(128)(2,1)} %get-tuple-element.429) | copy-start | bytes 3076
  323.0 128.8 %all-gather.11.cloned.1.call-start = ((), (), s32[]{:S(2)}) async-start(), calls=%async_computation.14 | async-start | bytes 3932160 | tf_op jit(solution)/shard_map/all_gather | solution.py:205
  388.1 136.9 %reduce-scatter.18.cloned.1.call-start = ((), (), s32[]{:S(2)}) async-start(), calls=%async_computation.15 | async-start | bytes 3932160 | tf_op jit(solution)/shard_map/reduce_scatter | solution.py:214
  451.8 10.4 %copy-start.33 = (bf16[512,512]{1,0:T(8,128)(2,1)S(1)}, bf16[512,512]{1,0:T(8,128)(2,1)}, u32[]{:S(2)}) copy-start(bf16[512,512]{1,0:T(8,128)(2,1)} %all_gather.70) | copy-start | bytes 1572868
  465.9 132.1 %all-gather.13.cloned.1.call-start = ((), (), s32[]{:S(2)}) async-start(), calls=%async_computation.16 | async-start | bytes 3932160 | tf_op jit(solution)/shard_map/all_gather | solution.py:227
  534.3 167.4 %reduce-scatter.32.cloned.1.call-start = ((), (), s32[]{:S(2)}) async-start(), calls=%async_computation.23 | async-start | bytes 589824 | tf_op jit(solution)/shard_map/reduce_scatter | solution.py:314
  539.9 163.3 %reduce-scatter.30.cloned.1.call-start = ((), (), s32[]{:S(2)}) async-start(), calls=%async_computation.22 | async-start | bytes 589824 | tf_op jit(solution)/shard_map/reduce_scatter | solution.py:308
  546.0 174.8 %reduce-scatter.28.cloned.1.call-start = ((), (), s32[]{:S(2)}) async-start(), calls=%async_computation.21 | async-start | bytes 147456 | tf_op jit(solution)/shard_map/reduce_scatter | solution.py:305
  686.5 68.8 %reduce-scatter.22.cloned.1.call-start = ((), (), s32[]{:S(2)}) async-start(), calls=%async_computation.18 | async-start | bytes 147456 | tf_op jit(solution)/shard_map/reduce_scatter | solution.py:290
  689.6 101.9 %reduce-scatter.26.cloned.1.call-start = ((), (), s32[]{:S(2)}) async-start(), calls=%async_computation.20 | async-start | bytes 147456 | tf_op jit(solution)/shard_map/reduce_scatter | solution.py:296
  692.5 135.7 %reduce-scatter.24.cloned.1.call-start = ((), (), s32[]{:S(2)}) async-start(), calls=%async_computation.19 | async-start | bytes 147456 | tf_op jit(solution)/shard_map/reduce_scatter | solution.py:293
  695.5 195.2 %reduce-scatter.20.cloned.1.call-start = ((), (), s32[]{:S(2)}) async-start(), calls=%async_computation.17 | async-start | bytes 3932160 | tf_op jit(solution)/shard_map/reduce_scatter | solution.py:259
  700.7 4.0 copy-start.52
  700.7 4.6 copy-start.21
  700.7 4.8 copy-start.22
  700.7 190.0 %copy-start.2 = (bf16[768,512]{1,0:T(8,128)(2,1)S(1)}, bf16[768,512]{1,0:T(8,128)(2,1)}, u32[]{:S(2)}) copy-start(bf16[768,512]{1,0:T(8,128)(2,1)} %param.28) | copy-start | bytes 2359300
  700.7 189.9 %copy-start.36 = (f32[768]{0:T(1024)S(1)}, f32[768]{0:T(1024)}, u32[]{:S(2)}) copy-start(f32[768]{0:T(1024)} %copy-done.35) | copy-start | bytes 9220
  700.7 189.9 %copy-start.43 = (f32[512]{0:T(512)S(1)}, f32[512]{0:T(512)}, u32[]{:S(2)}) copy-start(f32[512]{0:T(512)} %copy-done.42) | copy-start | bytes 6148
  700.8 191.7 %copy-start.45 = (f32[768]{0:T(1024)S(1)}, f32[768]{0:T(1024)}, u32[]{:S(2)}) copy-start(f32[768]{0:T(1024)} %copy-done.44) | copy-start | bytes 9220
  700.8 191.7 %copy-start.41 = (f32[768]{0:T(1024)S(1)}, f32[768]{0:T(1024)}, u32[]{:S(2)}) copy-start(f32[768]{0:T(1024)} %copy-done.40) | copy-start | bytes 9220
  705.5 187.9 %copy-start.53 = (f32[512]{0:T(512)S(1)}, f32[512]{0:T(512)}, u32[]{:S(2)}) copy-start(f32[512]{0:T(512)} %get-tuple-element.437) | copy-start | bytes 6148
  705.5 187.9 %copy-start.54 = (f32[512]{0:T(512)S(1)}, f32[512]{0:T(512)}, u32[]{:S(2)}) copy-start(f32[512]{0:T(512)} %get-tuple-element.338) | copy-start | bytes 6148
  705.5 187.9 %copy-start.55 = (f32[512]{0:T(512)S(1)}, f32[512]{0:T(512)}, u32[]{:S(2)}) copy-start(f32[512]{0:T(512)} %get-tuple-element.439) | copy-start | bytes 6148
  705.5 187.9 %copy-start.56 = (f32[512]{0:T(512)S(1)}, f32[512]{0:T(512)}, u32[]{:S(2)}) copy-start(f32[512]{0:T(512)} %get-tuple-element.343) | copy-start | bytes 6148
  705.5 233.4 %copy-start.11 = (f32[768,512]{1,0:T(8,128)S(1)}, f32[768,512]{1,0:T(8,128)}, u32[]{:S(2)}) copy-start(f32[768,512]{1,0:T(8,128)} %copy-done.10) | copy-start | bytes 4718596
  (43 other events, 80.6 us)
Sparse Core Ops, SparseCore 0:
  35.8 62.8 all-gather.6
  184.3 58.8 reduce-scatter.13
  246.8 63.5 all-gather.8
  323.2 59.8 reduce-scatter.15
  388.2 63.5 all-gather.10
  466.0 58.8 reduce-scatter.17
  534.4 63.5 all-gather.12
  601.1 32.8 reduce-scatter.31
  637.4 34.1 reduce-scatter.29
  686.6 31.9 reduce-scatter.27
  721.9 33.3 reduce-scatter.21
  758.2 33.3 reduce-scatter.25
  794.8 33.3 reduce-scatter.23
  830.4 60.2 reduce-scatter.19
where the time goes:
time: 957 us; the launch traced here: 949 us
  waiting for transfers between devices  458 us (48%)
  blocking collectives  194 us (20%)
  matrix products  117 us (12%)
  local copies, waits for them, and re-layouts  86.9 us (9%)
  other arithmetic  63 us (7%)
  between operations  19.7 us (2%)
    all_gather x1, waiting for transfers between devices, local(): grad_rows = lax.all_gather(grad_out_low, 'tp', axis=0, tiled=True)  63.5 us
    reduce_scatter x1, waiting for transfers between devices, local(): lax.psum_scatter(jnp.einsum('nc,dc->nd', stacked_grads, stacked_weights,...  61.1 us
    reduce_scatter x1, waiting for transfers between devices, local(): lax.psum_scatter(jnp.einsum('nf,df->nd', grad_pre, upper_w, preferred_ele...  59 us
    reduce_scatter x1, waiting for transfers between devices, local(): lax.psum_scatter(jnp.dot(attended, out_w, preferred_element_type=jnp.floa...  58.4 us
    all_gather x1, waiting for transfers between devices, local(): grad_attn_rows = lax.all_gather(grad_attn_low, 'tp', axis=0, tiled=True)  52 us
    psum x1, blocking collectives, local(): valid_total = lax.psum(jnp.sum(mask_float), ('fsdp', 'tp'))  42.1 us
    psum x1, blocking collectives, local(): lax.psum((square_part, grad_gain_first, grad_bias_first, grad_out_bias, g...  40.6 us
    reduce_scatter x1, waiting for transfers between devices, local(): lax.psum_scatter(grad_key_w.astype(jnp.bfloat16), 'fsdp', scatter_dimensi...  35.3 us
  transfers between devices with their start and end apart: 14, of which 11 were waited for; matrix products, arithmetic and copies ran while one was open for 13% of the time, Pallas kernels for 0%

commit v1 on v0

--- a/solution.py
+++ b/solution.py
@@ -183,7 +183,9 @@
     ).astype(jnp.float32)
     hidden_one = input_float + attention + out_b.astype(jnp.float32)
     normed_two = layer_norm(hidden_one, gain_second, bias_second).astype(jnp.bfloat16)
-    rows_two = lax.all_gather(normed_two, "tp", axis=0, tiled=True)
+    rows_two = jnp.concatenate(
+        lax.all_to_all(jnp.stack([normed_two] * lax.axis_size("tp")), "tp", 0, 0), axis=0
+    )
     pre_act = jnp.dot(rows_two, upper_w, preferred_element_type=jnp.float32) + upper_b.reshape(
         -1
     ).astype(jnp.float32)

time: 957 us -> 967 us (1.010)
    all_to_all x0 -> x1, waiting for transfers between devices: none -> 41 us  [local(): lax.all_to_all(jnp.stack([normed_two] * lax.axis_size('tp')), 'tp', 0, 0)]
    all_gather x1 -> x0, waiting for transfers between devices: 33.8 us -> none  [local(): rows_two = lax.all_gather(normed_two, 'tp', axis=0, tiled=True)]
where the time goes in v1:
time: 967 us; the launch traced here: 959 us
  waiting for transfers between devices  465 us (48%)
  blocking collectives  195 us (20%)
  matrix products  111 us (11%)
  local copies, waits for them, and re-layouts  91.8 us (9%)
  other arithmetic  62.1 us (6%)
  between operations  19.6 us (2%)
    all_gather x1, waiting for transfers between devices, local(): grad_rows = lax.all_gather(grad_out_low, 'tp', axis=0, tiled=True)  63.5 us
    reduce_scatter x1, waiting for transfers between devices, local(): lax.psum_scatter(jnp.einsum('nc,dc->nd', stacked_grads, stacked_weights,...  61.3 us
    reduce_scatter x1, waiting for transfers between devices, local(): lax.psum_scatter(jnp.einsum('nf,df->nd', grad_pre, upper_w, preferred_ele...  59 us
    reduce_scatter x1, waiting for transfers between devices, local(): lax.psum_scatter(jnp.dot(attended, out_w, preferred_element_type=jnp.floa...  58.4 us
    all_gather x1, waiting for transfers between devices, local(): grad_attn_rows = lax.all_gather(grad_attn_low, 'tp', axis=0, tiled=True)  52 us
    psum x1, blocking collectives, local(): valid_total = lax.psum(jnp.sum(mask_float), ('fsdp', 'tp'))  42.5 us
    all_to_all x1, waiting for transfers between devices, local(): lax.all_to_all(jnp.stack([normed_two] * lax.axis_size('tp')), 'tp', 0, 0)  41 us
    psum x1, blocking collectives, local(): lax.psum((square_part, grad_gain_first, grad_bias_first, grad_out_bias, g...  40.7 us
  transfers between devices with their start and end apart: 14, of which 11 were waited for; matrix products, arithmetic and copies ran while one was open for 13% of the time, Pallas kernels for 0%

profile of v1, /device:TPU:0, one launch (start us, length us, event | category | flops | bytes accessed | tf_op | source)
XLA Modules:
  0.0 959.0 jit_solution(1761160920472941449)
XLA Ops:
  14.4 16.0 %all-reduce.11 = (bf16[512]{0:T(512)(128)(2,1)}, bf16[512]{0:T(512)(128)(2,1)}, bf16[512]{0:T(512)(128)(2,1)}, bf16[512]{0:T(512)(128)(2,1)S(1)}, bf16[512]{0:T(512)(128)(2,1)S(1)}, /*index=5*/bf16[512]{0:T(512)(128)(2,1)}) all-reduce(bf16[512]{0:T(512)(128)(2,1)S(1)} %dynamic-update-slice.5, ...), channel_id=1, replica_groups=mesh['fsdp'=8,'tp'=4] {'fsdp'}, use_global_device_ids=true, to_apply=%add.5 | all-reduce | flops 3072 | bytes 12288
  35.8 7.7 all-gather
  43.7 8.8 all-gather.1
  52.6 8.2 all_gather.57
  60.8 9.3 all_gather.59
  70.1 8.2 all_gather.60
  78.2 10.2 %all_gather.62 = bf16[128,512]{0,1:T(8,128)(2,1)} all-gather(bf16[128,64]{0,1:T(8,128)(2,1)S(1)} %copy-done.50), channel_id=1, replica_groups=mesh['fsdp'=8,'tp'=4] {'fsdp'}, dimensions={1}, use_global_device_ids=true | all-gather | bytes 147456 | tf_op jit(solution)/shard_map/all_gather | solution.py:139
  88.5 10.3 %all-gather.6.cloned.1.call-done = bf16[3072,512]{1,0:T(8,128)(2,1)} async-done(((bf16[768,512]{1,0:T(8,128)(2,1)}), bf16[3072,512]{1,0:T(8,128)(2,1)}) %all-gather.6.cloned.1.call-update) | async-done | bytes 3145744 | tf_op jit(solution)/shard_map/all_gather | solution.py:158
  98.8 3.8 fusion.49
  102.5 4.2 reshape.355
  106.8 4.7 copy.106
  113.4 3.9 reshape.357
  117.2 4.7 copy.108
  123.9 4.0 reshape.356
  127.9 3.5 copy.107
  131.4 41.6 %while.54 = (s32[]{:T(128)}, bf16[3,2,512,2,64]{2,1,0,4,3:T(2,128)(2,1)}, f32[3,2,2,512]{3,2,1,0:T(2,128)}, bf16[3,2,512,2,64]{2,4,3,1,0:T(8,128)(2,1)S(1)}, s32...) while((s32[]{:T(128)}, ...), condition=%wide.region_7.8_spmd, body=%wide.region_2.7_spmd.sunk | while | flops 282656256 | bytes 17635796 | solution.py:174
  132.3 11.4 %while.57 = (s32[]{:T(128)}, bf16[2,512,2,64]{1,3,2,0:T(8,128)(2,1)S(1)}, f32[2,2,512]{2,1,0:T(2,128)S(1)}, s32[2]{0:T(128)S(1)}, s32[1024]{0:T(1024)S(1)}, /*in...) while((s32[]{:T(128)}, ...), condition=%wide.region_6.6_spmd, body=%wide.region_3.5_spmd.sunk | while | flops 282656256 | bytes 15513803 | solution.py:50
  146.1 11.5 %while.57 = (s32[]{:T(128)}, bf16[2,512,2,64]{1,3,2,0:T(8,128)(2,1)S(1)}, f32[2,2,512]{2,1,0:T(2,128)S(1)}, s32[2]{0:T(128)S(1)}, s32[1024]{0:T(1024)S(1)}, /*in...) while((s32[]{:T(128)}, ...), condition=%wide.region_6.6_spmd, body=%wide.region_3.5_spmd.sunk | while | flops 282656256 | bytes 15513803 | solution.py:50
  160.0 11.4 %while.57 = (s32[]{:T(128)}, bf16[2,512,2,64]{1,3,2,0:T(8,128)(2,1)S(1)}, f32[2,2,512]{2,1,0:T(2,128)S(1)}, s32[2]{0:T(128)S(1)}, s32[1024]{0:T(1024)S(1)}, /*in...) while((s32[]{:T(128)}, ...), condition=%wide.region_6.6_spmd, body=%wide.region_3.5_spmd.sunk | while | flops 282656256 | bytes 15513803 | solution.py:50
  179.7 58.4 %reduce-scatter.14.cloned.1.call-done = bf16[768,512]{1,0:T(8,128)(2,1)} async-done(((bf16[3072,512]{1,0:T(8,128)(2,1)}), bf16[768,512]{1,0:T(8,128)(2,1)}) %reduce-scatter.14.cloned.1.call-update) | async-done | bytes 786448 | tf_op jit(solution)/shard_map/reduce_scatter | solution.py:178
  242.5 4.8 all-to-all-start
  247.4 8.8 all_gather.67
  256.4 10.8 %all_gather.66 = bf16[512,512]{1,0:T(8,128)(2,1)} all-gather(bf16[64,512]{1,0:T(8,128)(2,1)S(1)} %copy-done.37), channel_id=1, replica_groups=mesh['fsdp'=8,'tp'=4] {'fsdp'}, dimensions={0}, use_global_device_ids=true | all-gather | bytes 589824 | tf_op jit(solution)/shard_map/all_gather | solution.py:143
  267.2 9.9 %all_gather.68 = bf16[512,512]{0,1:T(8,128)(2,1)} all-gather(bf16[512,64]{0,1:T(8,128)(2,1)S(1)} %copy-done.38), channel_id=1, replica_groups=mesh['fsdp'=8,'tp'=4] {'fsdp'}, dimensions={1}, use_global_device_ids=true | all-gather | bytes 589824 | tf_op jit(solution)/shard_map/all_gather | solution.py:145
  277.1 41.0 %all-to-all-done = bf16[4,768,512]{2,1,0:T(8,128)(2,1)} async-done(((bf16[4,768,512]{2,1,0:T(8,128)(2,1)}), bf16[4,768,512]{2,1,0:T(8,128)(2,1)}, u32[]{:S(2)}, u32[]{:S(2)}) %all-to-all-start) | async-done | bytes 3145760 | tf_op jit(solution)/shard_map/all_to_all | solution.py:187
  318.1 7.4 multiply_convert_fusion.1
  327.1 3.6 convolution_convert_fusion.2
  332.0 42.5 %psum.57 = f32[]{:T(128)} all-reduce(f32[]{:T(128)} %convert_reduce_fusion.3), channel_id=1, replica_groups=mesh['fsdp'=8,'tp'=4] {'fsdp','tp'}, use_global_device_ids=true, to_apply=%region_16.17 | all-reduce | flops 1 | bytes 8 | tf_op jit(solution)/shard_map/psum | solution.py:149
  375.2 16.0 %reduce-scatter.16.cloned.1.call-done = bf16[768,512]{1,0:T(8,128)(2,1)} async-done(((bf16[3072,512]{1,0:T(8,128)(2,1)}), bf16[768,512]{1,0:T(8,128)(2,1)}) %reduce-scatter.16.cloned.1.call-update) | async-done | bytes 786448 | tf_op jit(solution)/shard_map/reduce_scatter | solution.py:193
  396.4 63.5 %all-gather.8.cloned.1.call-done = bf16[3072,512]{1,0:T(8,128)(2,1)} async-done(((bf16[768,512]{1,0:T(8,128)(2,1)}), bf16[3072,512]{1,0:T(8,128)(2,1)}) %all-gather.8.cloned.1.call-update) | async-done | bytes 3145744 | tf_op jit(solution)/shard_map/all_gather | solution.py:207
  459.9 8.7 fusion.87
  470.3 3.6 convolution_convert_fusion.1
  474.0 59.0 %reduce-scatter.18.cloned.1.call-done = bf16[768,512]{1,0:T(8,128)(2,1)} async-done(((bf16[3072,512]{1,0:T(8,128)(2,1)}), bf16[768,512]{1,0:T(8,128)(2,1)}) %reduce-scatter.18.cloned.1.call-update) | async-done | bytes 786448 | tf_op jit(solution)/shard_map/reduce_scatter | solution.py:216
  542.5 5.5 convolution_convert_fusion.6
  548.0 6.0 convolution_convert_fusion.7
  554.1 52.0 %all-gather.10.cloned.1.call-done = bf16[3072,512]{1,0:T(8,128)(2,1)} async-done(((bf16[768,512]{1,0:T(8,128)(2,1)}), bf16[3072,512]{1,0:T(8,128)(2,1)}) %all-gather.10.cloned.1.call-update) | async-done | bytes 3145744 | tf_op jit(solution)/shard_map/all_gather | solution.py:229
  606.1 3.8 convolution_convert_fusion.4
  615.9 71.3 %while.56 = (s32[]{:T(128)}, bf16[3,2,512,2,64]{2,4,3,1,0:T(8,128)(2,1)}, bf16[3,1024,2,64]{1,3,2,0:T(8,128)(2,1)}, bf16[3,1024,2,64]{1,3,2,0:T(8,128)(2,1)}, bf...) while((s32[]{:T(128)}, ...), condition=%wide.region_24.25_spmd, body=%wide.region_20.24_spmd.sunk | while | flops 689438208 | bytes 45550196 | solution.py:236
  619.4 17.6 %while.58 = (s32[]{:T(128)}, f32[1024,2,64]{0,2,1:T(8,128)S(1)}, f32[1024,2,64]{0,2,1:T(8,128)}, bf16[2,512,2,64]{1,3,2,0:T(8,128)(2,1)S(1)}, bf16[2,512,2,64]{1...) while((s32[]{:T(128)}, f32[1024,2,64]{0,2,1:T(8,128)S(1)}, ...), condition=%wide.region_23.23_spmd.clone, body=%wide.region_21.22_spmd.clone.sunk | while | flops 689176064 | bytes 41330992 | solution.py:82
  643.1 17.6 %while.58 = (s32[]{:T(128)}, f32[1024,2,64]{0,2,1:T(8,128)S(1)}, f32[1024,2,64]{0,2,1:T(8,128)}, bf16[2,512,2,64]{1,3,2,0:T(8,128)(2,1)S(1)}, bf16[2,512,2,64]{1...) while((s32[]{:T(128)}, f32[1024,2,64]{0,2,1:T(8,128)S(1)}, ...), condition=%wide.region_23.23_spmd.clone, body=%wide.region_21.22_spmd.clone.sunk | while | flops 689176064 | bytes 41330992 | solution.py:82
  666.9 17.6 %while.58 = (s32[]{:T(128)}, f32[1024,2,64]{0,2,1:T(8,128)S(1)}, f32[1024,2,64]{0,2,1:T(8,128)}, bf16[2,512,2,64]{1,3,2,0:T(8,128)(2,1)S(1)}, bf16[2,512,2,64]{1...) while((s32[]{:T(128)}, f32[1024,2,64]{0,2,1:T(8,128)S(1)}, ...), condition=%wide.region_23.23_spmd.clone, body=%wide.region_21.22_spmd.clone.sunk | while | flops 689176064 | bytes 41330992 | solution.py:82
  705.8 5.1 convolution_convert_fusion
  716.0 13.7 %all-reduce.10 = (bf16[2,64]{1,0:T(2,128)(2,1)S(1)}, bf16[2,64]{1,0:T(2,128)(2,1)S(1)}, bf16[8,64]{1,0:T(8,128)(2,1)S(1)}) all-reduce(bf16[2,64]{1,0:T(2,128)(2,1)S(1)} %reduce_sum.233, bf16[2,64]{1,0:T(2,128)(2,1)S(1)} %reduce_sum.234, bf16[8,64]{1,0:T(8,128)(2,1)S(1)} %convert_element_type.247), channel_id=9, replica_groups=mesh['fsdp'=8,'tp'=4] {'fsdp'}, use_global_device_ids=true, to_apply=%region_36.37.clone | all-reduce | flops 768 | bytes 3072
  732.3 33.0 %reduce-scatter.22.cloned.1.call-done = bf16[64,128]{1,0:T(8,128)(2,1)} async-done(((bf16[512,128]{1,0:T(8,128)(2,1)}), bf16[64,128]{1,0:T(8,128)(2,1)}) %reduce-scatter.22.cloned.1.call-update) | async-done | bytes 16400 | tf_op jit(solution)/shard_map/reduce_scatter | solution.py:292
  766.7 35.1 %reduce-scatter.26.cloned.1.call-done = bf16[64,128]{1,0:T(8,128)(2,1)} async-done(((bf16[512,128]{1,0:T(8,128)(2,1)}), bf16[64,128]{1,0:T(8,128)(2,1)}) %reduce-scatter.26.cloned.1.call-update) | async-done | bytes 16400 | tf_op jit(solution)/shard_map/reduce_scatter | solution.py:298
  803.1 35.2 %reduce-scatter.24.cloned.1.call-done = bf16[64,128]{1,0:T(8,128)(2,1)} async-done(((bf16[512,128]{1,0:T(8,128)(2,1)}), bf16[64,128]{1,0:T(8,128)(2,1)}) %reduce-scatter.24.cloned.1.call-update) | async-done | bytes 16400 | tf_op jit(solution)/shard_map/reduce_scatter | solution.py:295
  839.6 61.3 %reduce-scatter.20.cloned.1.call-done = bf16[768,512]{1,0:T(8,128)(2,1)} async-done(((bf16[3072,512]{1,0:T(8,128)(2,1)}), bf16[768,512]{1,0:T(8,128)(2,1)}) %reduce-scatter.20.cloned.1.call-update) | async-done | bytes 786448 | tf_op jit(solution)/shard_map/reduce_scatter | solution.py:261
  903.7 40.7 %all-reduce.9 = (f32[]{:T(128)}, f32[512]{0:T(512)S(1)}, f32[512]{0:T(512)S(1)}, f32[512]{0:T(512)S(1)}, f32[512]{0:T(512)S(1)}, /*index=5*/f32[512]{0:T(512)S(1)}, f32[512]{0:T(512)S(1)}) all-reduce(f32[]{:T(128)} %multiply_reduce_fusion.3, f32[512]{0:T(512)S(1)} %get-tuple-element.340, ...), channel_id=1, replica_groups=mesh['fsdp'=8,'tp'=4] {'fsdp','tp'}, use_global_device_ids=true, to_apply=%region_14.15 | all-reduce | flops 3073 | bytes 24584 | tf_op jit(solution)/shard_map/psum | solution.py:272
  (448 shorter events, 193.8 us)
Async XLA Ops:
  7.2 27.3 %copy-start = (bf16[768,512]{1,0:T(8,128)(2,1)S(1)}, bf16[768,512]{1,0:T(8,128)(2,1)}, u32[]{:S(2)}) copy-start(bf16[768,512]{1,0:T(8,128)(2,1)} %param.28) | copy-start | bytes 2359300
  7.2 28.6 %copy-start.62 = (bf16[2,8]{1,0:T(2,128)(2,1)S(1)}, bf16[2,8]{1,0:T(2,128)(2,1)}, u32[]{:S(2)}) copy-start(bf16[2,8]{1,0:T(2,128)(2,1)} %param.38) | copy-start | bytes 100
  7.2 36.5 %copy-start.63 = (bf16[2,8]{1,0:T(2,128)(2,1)S(1)}, bf16[2,8]{1,0:T(2,128)(2,1)}, u32[]{:S(2)}) copy-start(bf16[2,8]{1,0:T(2,128)(2,1)} %param.39) | copy-start | bytes 100
  7.2 45.4 %copy-start.47 = (bf16[64,128]{1,0:T(8,128)(2,1)S(1)}, bf16[64,128]{1,0:T(8,128)(2,1)}, u32[]{:S(2)}) copy-start(bf16[64,128]{1,0:T(8,128)(2,1)} %param.35) | copy-start | bytes 49156
  7.2 91.5 %all-gather.6.cloned.1.call-start = ((), (), s32[]{:S(2)}) async-start(), calls=%async_computation.11 | async-start | bytes 3932160 | tf_op jit(solution)/shard_map/all_gather | solution.py:158
  30.4 30.4 %copy-start.48 = (bf16[64,128]{1,0:T(8,128)(2,1)S(1)}, bf16[64,128]{1,0:T(8,128)(2,1)}, u32[]{:S(2)}) copy-start(bf16[64,128]{1,0:T(8,128)(2,1)} %param.36) | copy-start | bytes 49156
  30.4 39.7 %copy-start.49 = (bf16[64,128]{1,0:T(8,128)(2,1)S(1)}, bf16[64,128]{1,0:T(8,128)(2,1)}, u32[]{:S(2)}) copy-start(bf16[64,128]{1,0:T(8,128)(2,1)} %param.37) | copy-start | bytes 49156
  30.4 47.8 %copy-start.50 = (bf16[128,64]{0,1:T(8,128)(2,1)S(1)}, bf16[128,64]{0,1:T(8,128)(2,1)}, u32[]{:S(2)}) copy-start(bf16[128,64]{0,1:T(8,128)(2,1)} %param.40) | copy-start | bytes 49156
  35.7 202.3 %reduce-scatter.14.cloned.1.call-start = ((), (), s32[]{:S(2)}) async-start(), calls=%async_computation.12 | async-start | bytes 3932160 | tf_op jit(solution)/shard_map/reduce_scatter | solution.py:178
  60.8 38.0 %copy-start.27 = (bf16[512,128]{1,0:T(8,128)(2,1)}, bf16[512,128]{1,0:T(8,128)(2,1)S(1)}, u32[]{:S(2)}) copy-start(bf16[512,128]{1,0:T(8,128)(2,1)S(1)} %all_gather.57) | copy-start | bytes 393220
  70.1 51.9 %copy-start.29 = (bf16[512,128]{1,0:T(8,128)(2,1)}, bf16[512,128]{1,0:T(8,128)(2,1)S(1)}, u32[]{:S(2)}) copy-start(bf16[512,128]{1,0:T(8,128)(2,1)S(1)} %all_gather.59) | copy-start | bytes 393220
  78.2 33.2 %copy-start.31 = (bf16[512,128]{1,0:T(8,128)(2,1)}, bf16[512,128]{1,0:T(8,128)(2,1)S(1)}, u32[]{:S(2)}) copy-start(bf16[512,128]{1,0:T(8,128)(2,1)S(1)} %all_gather.60) | copy-start | bytes 393220
  102.5 8.9 copy-start.3
  123.9 7.5 copy-start.7
  123.9 7.5 copy-start.8
  131.4 44.9 %copy-start.25 = (bf16[128,512]{0,1:T(8,128)(2,1)S(1)}, bf16[128,512]{0,1:T(8,128)(2,1)}, u32[]{:S(2)}) copy-start(bf16[128,512]{0,1:T(8,128)(2,1)} %all_gather.62) | copy-start | bytes 393220
  178.9 59.1 %copy-start.1 = (bf16[768,512]{1,0:T(8,128)(2,1)S(1)}, bf16[768,512]{1,0:T(8,128)(2,1)}, u32[]{:S(2)}) copy-start(bf16[768,512]{1,0:T(8,128)(2,1)} %param.28) | copy-start | bytes 2359300
  242.5 4.8 copy-start.56
  242.5 13.9 %copy-start.37 = (bf16[64,512]{1,0:T(8,128)(2,1)S(1)}, bf16[64,512]{1,0:T(8,128)(2,1)}, u32[]{:S(2)}) copy-start(bf16[64,512]{1,0:T(8,128)(2,1)} %param.44) | copy-start | bytes 196612
  242.5 24.7 %copy-start.38 = (bf16[512,64]{0,1:T(8,128)(2,1)S(1)}, bf16[512,64]{0,1:T(8,128)(2,1)}, u32[]{:S(2)}) copy-start(bf16[512,64]{0,1:T(8,128)(2,1)} %param.46) | copy-start | bytes 196612
  242.5 75.6 %all-to-all-start = ((bf16[4,768,512]{2,1,0:T(8,128)(2,1)}), bf16[4,768,512]{2,1,0:T(8,128)(2,1)}, u32[]{:S(2)}, u32[]{:S(2)}) async-start(bf16[4,768,512]{2,1,0:T(8,128)(2,1)} %stack.2), calls=%async_computation.1 | async-start | bytes 6291456 | tf_op jit(solution)/shard_map/all_to_all | solution.py:187
  247.3 143.9 %reduce-scatter.16.cloned.1.call-start = ((), (), s32[]{:S(2)}) async-start(), calls=%async_computation.13 | async-start | bytes 3932160 | tf_op jit(solution)/shard_map/reduce_scatter | solution.py:193
  318.1 9.0 copy-start.34
  330.8 43.7 %copy-start.58 = (bf16[512]{0:T(512)(128)(2,1)S(1)}, bf16[512]{0:T(512)(128)(2,1)}, u32[]{:S(2)}) copy-start(bf16[512]{0:T(512)(128)(2,1)} %get-tuple-element.429) | copy-start | bytes 3076
  330.8 129.2 %all-gather.8.cloned.1.call-start = ((), (), s32[]{:S(2)}) async-start(), calls=%async_computation.14 | async-start | bytes 3932160 | tf_op jit(solution)/shard_map/all_gather | solution.py:207
  396.2 136.8 %reduce-scatter.18.cloned.1.call-start = ((), (), s32[]{:S(2)}) async-start(), calls=%async_computation.15 | async-start | bytes 3932160 | tf_op jit(solution)/shard_map/reduce_scatter | solution.py:216
  459.9 10.4 %copy-start.33 = (bf16[512,512]{1,0:T(8,128)(2,1)S(1)}, bf16[512,512]{1,0:T(8,128)(2,1)}, u32[]{:S(2)}) copy-start(bf16[512,512]{1,0:T(8,128)(2,1)} %all_gather.66) | copy-start | bytes 1572868
  474.0 132.1 %all-gather.10.cloned.1.call-start = ((), (), s32[]{:S(2)}) async-start(), calls=%async_computation.16 | async-start | bytes 3932160 | tf_op jit(solution)/shard_map/all_gather | solution.py:229
  542.4 169.5 %reduce-scatter.32.cloned.1.call-start = ((), (), s32[]{:S(2)}) async-start(), calls=%async_computation.23 | async-start | bytes 589824 | tf_op jit(solution)/shard_map/reduce_scatter | solution.py:316
  548.0 165.4 %reduce-scatter.30.cloned.1.call-start = ((), (), s32[]{:S(2)}) async-start(), calls=%async_computation.22 | async-start | bytes 589824 | tf_op jit(solution)/shard_map/reduce_scatter | solution.py:310
  554.0 176.9 %reduce-scatter.28.cloned.1.call-start = ((), (), s32[]{:S(2)}) async-start(), calls=%async_computation.21 | async-start | bytes 147456 | tf_op jit(solution)/shard_map/reduce_scatter | solution.py:307
  696.6 68.7 %reduce-scatter.22.cloned.1.call-start = ((), (), s32[]{:S(2)}) async-start(), calls=%async_computation.18 | async-start | bytes 147456 | tf_op jit(solution)/shard_map/reduce_scatter | solution.py:292
  699.8 102.0 %reduce-scatter.26.cloned.1.call-start = ((), (), s32[]{:S(2)}) async-start(), calls=%async_computation.20 | async-start | bytes 147456 | tf_op jit(solution)/shard_map/reduce_scatter | solution.py:298
  702.7 135.6 %reduce-scatter.24.cloned.1.call-start = ((), (), s32[]{:S(2)}) async-start(), calls=%async_computation.19 | async-start | bytes 147456 | tf_op jit(solution)/shard_map/reduce_scatter | solution.py:295
  705.7 195.2 %reduce-scatter.20.cloned.1.call-start = ((), (), s32[]{:S(2)}) async-start(), calls=%async_computation.17 | async-start | bytes 3932160 | tf_op jit(solution)/shard_map/reduce_scatter | solution.py:261
  710.9 4.0 copy-start.51
  710.9 4.6 copy-start.21
  710.9 4.8 copy-start.22
  710.9 190.0 %copy-start.2 = (bf16[768,512]{1,0:T(8,128)(2,1)S(1)}, bf16[768,512]{1,0:T(8,128)(2,1)}, u32[]{:S(2)}) copy-start(bf16[768,512]{1,0:T(8,128)(2,1)} %param.28) | copy-start | bytes 2359300
  710.9 190.0 %copy-start.36 = (f32[768]{0:T(1024)S(1)}, f32[768]{0:T(1024)}, u32[]{:S(2)}) copy-start(f32[768]{0:T(1024)} %copy-done.35) | copy-start | bytes 9220
  710.9 190.0 %copy-start.42 = (f32[512]{0:T(512)S(1)}, f32[512]{0:T(512)}, u32[]{:S(2)}) copy-start(f32[512]{0:T(512)} %copy-done.41) | copy-start | bytes 6148
  711.0 191.7 %copy-start.44 = (f32[768]{0:T(1024)S(1)}, f32[768]{0:T(1024)}, u32[]{:S(2)}) copy-start(f32[768]{0:T(1024)} %copy-done.43) | copy-start | bytes 9220
  711.0 191.7 %copy-start.40 = (f32[768]{0:T(1024)S(1)}, f32[768]{0:T(1024)}, u32[]{:S(2)}) copy-start(f32[768]{0:T(1024)} %copy-done.39) | copy-start | bytes 9220
  715.7 187.9 %copy-start.52 = (f32[512]{0:T(512)S(1)}, f32[512]{0:T(512)}, u32[]{:S(2)}) copy-start(f32[512]{0:T(512)} %get-tuple-element.437) | copy-start | bytes 6148
  715.7 187.9 %copy-start.53 = (f32[512]{0:T(512)S(1)}, f32[512]{0:T(512)}, u32[]{:S(2)}) copy-start(f32[512]{0:T(512)} %get-tuple-element.338) | copy-start | bytes 6148
  715.7 187.9 %copy-start.54 = (f32[512]{0:T(512)S(1)}, f32[512]{0:T(512)}, u32[]{:S(2)}) copy-start(f32[512]{0:T(512)} %get-tuple-element.439) | copy-start | bytes 6148
  715.7 187.9 %copy-start.55 = (f32[512]{0:T(512)S(1)}, f32[512]{0:T(512)}, u32[]{:S(2)}) copy-start(f32[512]{0:T(512)} %get-tuple-element.343) | copy-start | bytes 6148
  715.8 233.4 %copy-start.11 = (f32[768,512]{1,0:T(8,128)S(1)}, f32[768,512]{1,0:T(8,128)}, u32[]{:S(2)}) copy-start(f32[768,512]{1,0:T(8,128)} %copy-done.10) | copy-start | bytes 4718596
  (42 other events, 79.1 us)
Sparse Core Ops, SparseCore 0:
  35.8 62.8 all-gather.5
  179.1 58.8 reduce-scatter.13
  330.9 60.2 reduce-scatter.15
  396.3 63.5 all-gather.7
  474.1 58.8 reduce-scatter.17
  542.5 63.5 all-gather.9
  609.1 32.8 reduce-scatter.31
  645.4 34.0 reduce-scatter.29
  696.8 32.0 reduce-scatter.27
  732.0 33.3 reduce-scatter.21
  768.4 33.3 reduce-scatter.25
  804.9 33.3 reduce-scatter.23
  840.6 60.2 reduce-scatter.19
